TPU v7x, 512 devices: a whole 4x4x16 slice. The times are simulated.
512 devices in a mesh: lat: 4 (over x_hi, core), lon: 32 (over z, x_lo), tensor: 4 (over y).
Axes of the slice: x: 4 (x_hi: 2, x_lo: 2; x = x_hi * 2 + x_lo), y: 4, z: 16, core: 2. Of those that a mesh axis runs over, the one named last changes fastest.
Arguments:
- fields: bfloat16 [64, 768, 256], P('lat', 'lon'), may hold values from -8 to 8
- norm_gain1: float32 [256], replicated, may hold values from 0.5 to 1.5
- w_qkv: bfloat16 [256, 3, 8, 32], P(None, None, 'tensor'), may hold values from -0.1875 to 0.1875
- logit_scale: float32 [8], P('tensor'), may hold values from 1 to 64
- w_out: bfloat16 [8, 32, 256], P('tensor'), may hold values from -0.375 to 0.375
- attn_keep: int32 [64, 256], P('lat'), may hold values 0 or 1
- dw_kernel: bfloat16 [7, 7, 256], replicated, may hold values from -0.875 to 0.875
- norm_gain2: float32 [256], replicated, may hold values from 0.5 to 1.5
- w_up: bfloat16 [256, 1024], P(None, 'tensor'), may hold values from -0.375 to 0.375
- w_down: bfloat16 [1024, 256], P('tensor'), may hold values from -0.1875 to 0.1875
- mlp_keep: int32 [64, 256], P('lat'), may hold values 0 or 1
Outputs:
- result: bfloat16 [64, 768, 256], P('lat', 'lon')
All inputs are finite; a program needn't handle non-finite values. No bound on the sum of `attn_keep` or of `mlp_keep` on one device may be relied on, other than what follows from the above.
Results may differ from a plain program's by a relative error of at most 0.014.
Values may be sent and summed in bfloat16 or wider, within the bound.
A program may use at most 64 MiB of HBM per device.

v0:
```python
import math
import jax
import jax.numpy as jnp
from jax import lax
from jax.sharding import PartitionSpec as P

ln_eps = 1e-05
keep_prob = 0.9


def padded(shard, sides, width, wrap):
    for axis, dim in sides:
        size, length = (lax.axis_size(axis), shard.shape[dim])
        up = [(i, (i + 1) % size) for i in range(size if wrap else size - 1)]
        down = [(j, i) for i, j in up]
        last = lax.slice_in_dim(shard, length - width, length, axis=dim)
        first = lax.slice_in_dim(shard, 0, width, axis=dim)
        before = lax.ppermute(last, axis, up)
        after = lax.ppermute(first, axis, down)
        shard = jnp.concatenate([before, shard, after], axis=dim)
    return shard


def layer_norm(values, gain):
    widened = values.astype(jnp.float32)
    center = jnp.mean(widened, axis=-1, keepdims=True)
    spread = jnp.mean(jnp.square(widened - center), axis=-1, keepdims=True)
    return (widened - center) * lax.rsqrt(spread + ln_eps) * gain


def depthwise(wide, kernel, rows, cols):
    kernel_f = kernel.astype(jnp.float32)
    wide_f = wide.astype(jnp.float32)
    width = kernel.shape[0]
    total = jnp.zeros((rows, cols, wide.shape[2]), jnp.float32)
    for row_off in range(width):
        for col_off in range(width):
            total = (
                total
                + kernel_f[row_off, col_off]
                * wide_f[row_off : row_off + rows, col_off : col_off + cols]
            )
    return total


def widen(stream, margin):
    rows_wide = padded(stream, (("lat", 0),), margin, False)
    return padded(rows_wide, (("lon", 1),), margin, True)


def feed_forward(spatial, norm_gain2, w_up, w_down):
    normed2 = layer_norm(spatial, norm_gain2).astype(jnp.bfloat16)
    hidden = jax.nn.gelu(
        jnp.einsum("rlc,cf->rlf", normed2, w_up, preferred_element_type=jnp.float32),
        approximate=False,
    ).astype(jnp.bfloat16)
    return jnp.einsum("rlf,fc->rlc", hidden, w_down, preferred_element_type=jnp.float32)


def shards(
    fields,
    norm_gain1,
    w_qkv,
    logit_scale,
    w_out,
    attn_keep,
    dw_kernel,
    norm_gain2,
    w_up,
    w_down,
    mlp_keep,
):
    lat_rows, lon_cols, channels = fields.shape
    local_heads = w_qkv.shape[2]
    head_size = w_qkv.shape[3]
    logit_coef = logit_scale * (1.0 / math.sqrt(head_size))
    normed = layer_norm(fields, norm_gain1).astype(jnp.bfloat16)
    projected = jnp.einsum(
        "rlc,cjhd->rljhd", normed, w_qkv, preferred_element_type=jnp.float32
    ).astype(jnp.bfloat16)
    queries = projected[:, :, 0]
    keys_values = projected[:, :, 1:].reshape(lat_rows, lon_cols, 2 * local_heads * head_size)
    piece = lax.all_gather(keys_values, "lon", axis=1, tiled=True)
    running_max = jnp.full((lat_rows, local_heads, lon_cols), -1e30, jnp.float32)
    count = piece.shape[1]
    split_piece = piece.reshape(lat_rows, count, 2, local_heads, head_size)
    scores = jnp.einsum(
        "rqhd,rkhd->rhqk", queries, split_piece[:, :, 0], preferred_element_type=jnp.float32
    )
    scores = scores * logit_coef[None, :, None, None]
    new_max = jnp.maximum(running_max, jnp.max(scores, axis=-1))
    weights = jnp.exp(scores - new_max[..., None])
    new_sum = jnp.sum(weights, axis=-1)
    gathered = jnp.einsum(
        "rhqk,rkhd->rhqd",
        weights.astype(jnp.bfloat16),
        split_piece[:, :, 1],
        preferred_element_type=jnp.float32,
    )
    mixed = (gathered / new_sum[..., None]).astype(jnp.bfloat16)
    partial_value = jnp.einsum("rhqd,hdc->rqc", mixed, w_out, preferred_element_type=jnp.float32)
    attended = lax.psum(partial_value.astype(jnp.bfloat16), "tensor").astype(jnp.float32)
    attn_factor = (attn_keep.astype(jnp.float32) / keep_prob)[:, None, :]
    mlp_factor = (mlp_keep.astype(jnp.float32) / keep_prob)[:, None, :]
    margin = dw_kernel.shape[0] // 2
    stream = (fields.astype(jnp.float32) + attended * attn_factor).astype(jnp.bfloat16)
    spatial = depthwise(widen(stream, margin), dw_kernel, lat_rows, lon_cols).astype(jnp.bfloat16)
    ffn_sum = lax.psum(
        feed_forward(spatial, norm_gain2, w_up, w_down).astype(jnp.bfloat16), "tensor"
    ).astype(jnp.float32)
    result = (stream.astype(jnp.float32) + ffn_sum * mlp_factor).astype(jnp.bfloat16)
    return result


def solution(mesh):
    placed = (
        P("lat", "lon", None),
        P(),
        P(None, None, "tensor", None),
        P("tensor"),
        P("tensor", None, None),
        P("lat", None),
        P(),
        P(),
        P(None, "tensor"),
        P("tensor", None),
        P("lat", None),
    )
    return jax.shard_map(
        shards, mesh=mesh, in_specs=placed, out_specs=P("lat", "lon", None), check_vma=False
    )
```

profile of v0, /device:TPU:2, one launch (start us, length us, event | category | flops | bytes accessed | tf_op | source)
XLA Modules:
  0.0 309.6 jit_solution(4489916328786344057)
XLA Ops:
  6.5 0.0 copy-start
  6.5 0.0 all-gather.2.cloned.1.call-start
  6.5 1.1 convert_reduce_fusion
  7.7 1.2 fusion.18
  8.8 1.4 convolution_convert_fusion
  10.3 0.3 copy.12
  10.6 0.9 reshape.39
  11.5 0.0 all-gather.2.cloned.1.call-update
  11.5 0.0 all-reduce.3.cloned.1.call-start
  11.5 0.0 copy-done.8
  11.6 0.0 copy-done.3
  11.6 140.8 %all-gather.2.cloned.1.call-done = bf16[16,768,128]{2,1,0:T(8,128)(2,1)} async-done(((bf16[16,24,128]{2,1,0:T(8,128)(2,1)}), bf16[16,768,128]{2,1,0:T(8,128)(2,1)}) %all-gather.2.cloned.1.call-update) | async-done | bytes 3145744 | tf_op jit(solution)/shard_map/all_gather | solution.py:83
  152.4 4.7 %copy.13 = bf16[16,768,128]{1,2,0:T(8,128)(2,1)} copy(bf16[16,768,128]{2,1,0:T(8,128)(2,1)} %all-gather.2.cloned.1.call-done) | data formatting | bytes 6291456 | tf_op jit(solution)/shard_map/all_gather | solution.py:83
  157.1 2.0 multiply_reduce_fusion
  159.0 0.6 fusion
  159.6 0.0 copy-done.6
  159.7 0.0 copy-start.2
  159.7 0.0 copy-start.1
  159.7 3.2 %fusion.11 = bf16[16,24,256]{2,1,0:T(8,128)(2,1)} fusion(bf16[16,768,2,2,32]{1,4,3,2,0:T(8,128)(2,1)} %bitcast.96, f32[16,2,24,768]{3,2,1,0:T(8,128)S(1)} %get-tuple-element.63, f32[16,2,24]{2,1,0:T(2,128)S(1)} %broadcast_maximum_fusion, f32[2]{0:T(128)S(1)} %broadcast_multiply_fusion.2, f32[16,2,24]{2,1,0:T(2,128)S(1)} %fusion, ...), kind=kOutput, calls=%fused_computation.14 | convolution fusion | flops 52248576 | bytes 4167688 | tf_op jit(solution)/shard_map/rhqd,hdc->rqc/dot_general | solution.py:101
  162.9 0.0 all-reduce.3.cloned.1.call-update
  162.9 0.0 all-reduce.5.cloned.1.call-start
  163.0 0.0 copy-done.2
  163.0 54.8 %all-reduce.3.cloned.1.call-done = bf16[16,24,256]{2,1,0:T(8,128)(2,1)} async-done(((bf16[16,24,256]{2,1,0:T(8,128)(2,1)}), bf16[16,24,256]{2,1,0:T(8,128)(2,1)}) %all-reduce.3.cloned.1.call-update) | async-done | bytes 196624 | tf_op jit(solution)/shard_map/psum | solution.py:102
  217.8 0.0 copy-done.1
  217.8 1.0 fusion.24
  218.8 1.3 collective-permute-start
  220.1 1.3 collective-permute-start.1
  221.5 0.0 collective-permute-done
  221.5 4.1 %collective-permute-done.1 = bf16[3,24,256]{2,1,0:T(8,128)(2,1)S(1)} collective-permute-done((bf16[3,24,256]{2,1,0:T(8,128)(2,1)S(1)}, bf16[3,24,256]{2,1,0:T(8,128)(2,1)S(1)}, u32[]{:S(2)}, u32[]{:S(2)}) %collective-permute-start.1) | collective-permute-done | bytes 36896 | tf_op jit(solution)/shard_map/ppermute | solution.py:19
  225.6 4.4 %collective-permute-start.2 = (bf16[22,3,256]{2,1,0:T(4,128)(2,1)S(1)}, bf16[22,3,256]{2,1,0:T(4,128)(2,1)S(1)}, u32[]{:S(2)}, u32[]{:S(2)}) collective-permute-start(bf16[22,3,256]{2,1,0:T(4,128)(2,1)S(1)} %get-tuple-element.9), channel_id=1, source_target_pairs={{0,4},{4,8},{8,12},{12,16},{16,20},{20,24},{24,28},{28,32},{32,36}... | collective-permute-start | bytes 101384 | tf_op jit(solution)/shard_map/ppermute | solution.py:18
  230.0 1.9 collective-permute-start.3
  231.9 0.0 collective-permute-done.2
  231.9 4.9 %collective-permute-done.3 = bf16[22,3,256]{2,1,0:T(4,128)(2,1)S(1)} collective-permute-done((bf16[22,3,256]{2,1,0:T(4,128)(2,1)S(1)}, bf16[22,3,256]{2,1,0:T(4,128)(2,1)S(1)}, u32[]{:S(2)}, u32[]{:S(2)}) %collective-permute-start.3) | collective-permute-done | bytes 33824 | tf_op jit(solution)/shard_map/ppermute | solution.py:19
  236.8 0.1 maximum_convert_fusion
  236.9 0.0 copy-start.7
  237.0 0.0 copy-start.5
  237.0 2.9 convert_reduce_fusion.1
  239.9 0.2 fusion.21
  240.1 0.0 copy-done
  240.2 0.0 copy-done.7
  240.2 0.3 fusion.95
  240.5 0.0 copy-done.5
  240.5 0.0 copy-start.4
  240.5 1.8 convolution_convert_fusion.1
  242.3 0.0 all-reduce.5.cloned.1.call-update
  242.3 0.0 copy-done.4
  242.3 59.0 %all-reduce.5.cloned.1.call-done = bf16[16,24,256]{2,1,0:T(8,128)(2,1)} async-done(((bf16[16,24,256]{2,1,0:T(8,128)(2,1)}), bf16[16,24,256]{2,1,0:T(8,128)(2,1)}) %all-reduce.5.cloned.1.call-update) | async-done | bytes 196624 | tf_op jit(solution)/shard_map/psum | solution.py:108
  301.4 1.7 add_convert_fusion
  (17 shorter events, 0.2 us)
Async XLA Ops:
  6.5 233.6 %copy-start = (bf16[256,256]{1,0:T(8,128)(2,1)S(1)}, bf16[256,256]{1,0:T(8,128)(2,1)}, u32[]{:S(2)}) copy-start(bf16[256,256]{1,0:T(8,128)(2,1)} %param.19) | copy-start | bytes 393220
  6.5 5.0 %copy-start.8 = (f32[2]{0:T(128)S(1)}, f32[2]{0:T(128)}, u32[]{:S(2)}) copy-start(f32[2]{0:T(128)} %param.14) | copy-start | bytes 28
  6.5 5.0 %copy-start.3 = (s32[16,256]{1,0:T(8,128)S(1)}, s32[16,256]{1,0:T(8,128)}, u32[]{:S(2)}) copy-start(s32[16,256]{1,0:T(8,128)} %param.16) | copy-start | bytes 49156
  6.5 145.8 %all-gather.2.cloned.1.call-start = ((), (), s32[]{:S(2)}) async-start(), calls=%async_computation | async-start | bytes 3244032 | tf_op jit(solution)/shard_map/all_gather | solution.py:83
  11.5 206.3 %all-reduce.3.cloned.1.call-start = ((), (), s32[]{:S(2)}) async-start(), calls=%async_computation.1 | async-start | bytes 393216 | tf_op jit(solution)/shard_map/psum | solution.py:102
  157.0 2.6 copy-start.6
  159.7 3.3 %copy-start.2 = (bf16[7,7,256]{2,1,0:T(8,128)(2,1)S(1)}, bf16[7,7,256]{2,1,0:T(8,128)(2,1)}, u32[]{:S(2)}) copy-start(bf16[7,7,256]{2,1,0:T(8,128)(2,1)} %param.17) | copy-start | bytes 75268
  159.7 58.2 %copy-start.1 = (bf16[16,24,256]{2,1,0:T(8,128)(2,1)S(1)}, bf16[16,24,256]{2,1,0:T(8,128)(2,1)}, u32[]{:S(2)}) copy-start(bf16[16,24,256]{2,1,0:T(8,128)(2,1)} %param.11) | copy-start | bytes 589828
  162.9 138.5 %all-reduce.5.cloned.1.call-start = ((), (), s32[]{:S(2)}) async-start(), calls=%async_computation.2 | async-start | bytes 393216 | tf_op jit(solution)/shard_map/psum | solution.py:108
  218.8 2.6 collective-permute-start
  220.1 5.4 %collective-permute-start.1 = (bf16[3,24,256]{2,1,0:T(8,128)(2,1)S(1)}, bf16[3,24,256]{2,1,0:T(8,128)(2,1)S(1)}, u32[]{:S(2)}, u32[]{:S(2)}) collective-permute-start(bf16[3,24,256]{2,1,0:T(8,128)(2,1)S(1)} %get-tuple-element.12), channel_id=1, source_target_pairs={{128,0},{256,128},{384,256},{129,1},{257,129},{385,257},{130,2},{2... | collective-permute-start | bytes 110600 | tf_op jit(solution)/shard_map/ppermute | solution.py:19
  225.6 6.3 %collective-permute-start.2 = (bf16[22,3,256]{2,1,0:T(4,128)(2,1)S(1)}, bf16[22,3,256]{2,1,0:T(4,128)(2,1)S(1)}, u32[]{:S(2)}, u32[]{:S(2)}) collective-permute-start(bf16[22,3,256]{2,1,0:T(4,128)(2,1)S(1)} %get-tuple-element.9), channel_id=1, source_target_pairs={{0,4},{4,8},{8,12},{12,16},{16,20},{20,24},{24,28},{28,32},{32,36}... | collective-permute-start | bytes 101384 | tf_op jit(solution)/shard_map/ppermute | solution.py:18
  230.0 6.8 %collective-permute-start.3 = (bf16[22,3,256]{2,1,0:T(4,128)(2,1)S(1)}, bf16[22,3,256]{2,1,0:T(4,128)(2,1)S(1)}, u32[]{:S(2)}, u32[]{:S(2)}) collective-permute-start(bf16[22,3,256]{2,1,0:T(4,128)(2,1)S(1)} %get-tuple-element.10), channel_id=1, source_target_pairs={{4,0},{8,4},{12,8},{16,12},{20,16},{24,20},{28,24},{32,28},{36,32}... | collective-permute-start | bytes 101384 | tf_op jit(solution)/shard_map/ppermute | solution.py:19
  236.9 3.2 %copy-start.7 = (f32[256]{0:T(256)S(1)}, f32[256]{0:T(256)}, u32[]{:S(2)}) copy-start(f32[256]{0:T(256)} %param.18) | copy-start | bytes 3076
  237.0 3.6 %copy-start.5 = (bf16[256,256]{1,0:T(8,128)(2,1)S(1)}, bf16[256,256]{1,0:T(8,128)(2,1)}, u32[]{:S(2)}) copy-start(bf16[256,256]{1,0:T(8,128)(2,1)} %param.20) | copy-start | bytes 393220
  240.5 1.8 copy-start.4
Sparse Core Ops, SparseCore 0:
  11.6 140.6 all-gather.1
  163.0 54.7 all-reduce.2
  242.4 58.8 all-reduce.4
where the time goes:
time: 310 us
  waiting for transfers between devices  264 us (85%)
  between operations  13.4 us (4%)
  starting transfers between devices  8.95 us (3%)
  other arithmetic  8.84 us (3%)
  matrix products  8.69 us (3%)
  local copies, waits for them, and re-layouts  6.01 us (2%)
    all_gather x1, waiting for transfers between devices, shards(): piece = lax.all_gather(keys_values, 'lon', axis=1, tiled=True)  141 us
    psum x1, waiting for transfers between devices, shards(): lax.psum(feed_forward(spatial, norm_gain2, w_up, w_down).astype(jnp.bfloa...  59 us
    psum x1, waiting for transfers between devices, shards(): lax.psum(partial_value.astype(jnp.bfloat16), 'tensor').astype(jnp.float32)  54.8 us
    ppermute x2, waiting for transfers between devices, padded(): after = lax.ppermute(first, axis, down)  8.96 us
  transfers between devices with their start and end apart: 7, of which 5 were waited for; matrix products, arithmetic and copies ran while one was open for 0% of the time, Pallas kernels for 0%

commit v1 on v0

--- a/solution.py
+++ b/solution.py
@@ -99,7 +99,9 @@
     )
     mixed = (gathered / new_sum[..., None]).astype(jnp.bfloat16)
     partial_value = jnp.einsum("rhqd,hdc->rqc", mixed, w_out, preferred_element_type=jnp.float32)
-    attended = lax.psum(partial_value.astype(jnp.bfloat16), "tensor").astype(jnp.float32)
+    attended = jnp.sum(lax.all_gather(partial_value.astype(jnp.bfloat16), "tensor"), axis=0).astype(
+        jnp.float32
+    )
     attn_factor = (attn_keep.astype(jnp.float32) / keep_prob)[:, None, :]
     mlp_factor = (mlp_keep.astype(jnp.float32) / keep_prob)[:, None, :]
     margin = dw_kernel.shape[0] // 2

time: 310 us -> 264 us (0.85)
  waiting for transfers between devices: 264 us -> 206 us
  blocking collectives: 0 us -> 13.4 us
    psum x1 -> x0, waiting for transfers between devices: 54.8 us -> none  [shards(): lax.psum(partial_value.astype(jnp.bfloat16), 'tensor').astype(jnp.float32)]
    all_gather x0 -> x1, blocking collectives: none -> 13.4 us  [shards(): lax.all_gather(partial_value.astype(jnp.bfloat16), 'tensor')]
    psum x1, waiting for transfers between devices: 59 us -> 55.8 us  [shards(): lax.psum(feed_forward(spatial, norm_gain2, w_up, w_down).astype(jnp.bfloa...]
  transfers between devices with their start and end apart: 7 -> 6, of which waited for: 5 -> 4; matrix products, arithmetic and copies ran while one was open for 0% -> 0% of each run, Pallas kernels for 0% -> 0%
where the time goes in v1:
time: 264 us
  waiting for transfers between devices  206 us (78%)
  between operations  13.7 us (5%)
  blocking collectives  13.4 us (5%)
  starting transfers between devices  9.03 us (3%)
  other arithmetic  8.05 us (3%)
  matrix products  7.99 us (3%)
  local copies, waits for them, and re-layouts  6.01 us (2%)
    all_gather x1, waiting for transfers between devices, shards(): piece = lax.all_gather(keys_values, 'lon', axis=1, tiled=True)  141 us
    psum x1, waiting for transfers between devices, shards(): lax.psum(feed_forward(spatial, norm_gain2, w_up, w_down).astype(jnp.bfloa...  55.8 us
    all_gather x1, blocking collectives, shards(): lax.all_gather(partial_value.astype(jnp.bfloat16), 'tensor')  13.4 us
    ppermute x2, waiting for transfers between devices, padded(): after = lax.ppermute(first, axis, down)  9.23 us
    ppermute x2, starting transfers between devices, padded(): before = lax.ppermute(last, axis, up)  5.74 us
  transfers between devices with their start and end apart: 6, of which 4 were waited for; matrix products, arithmetic and copies ran while one was open for 0% of the time, Pallas kernels for 0%

profile of v1, /device:TPU:2, one launch (start us, length us, event | category | flops | bytes accessed | tf_op | source)
XLA Modules:
  0.0 264.0 jit_solution(16548858310695219353)
XLA Ops:
  6.5 0.0 copy-start
  6.5 0.0 copy-start.8
  6.5 0.0 copy-start.2
  6.5 0.0 all-gather.3.cloned.1.call-start
  6.6 1.1 convert_reduce_fusion
  7.7 1.2 fusion.18
  8.9 1.4 convolution_convert_fusion
  10.3 0.3 copy.15
  10.6 0.9 reshape.39
  11.5 0.0 all-gather.3.cloned.1.call-update
  11.5 0.0 all-reduce.2.cloned.1.call-start
  11.6 0.0 copy-done.8
  11.6 0.0 copy-done.2
  11.6 0.0 copy-done.3
  11.7 140.7 %all-gather.3.cloned.1.call-done = bf16[16,768,128]{2,1,0:T(8,128)(2,1)} async-done(((bf16[16,24,128]{2,1,0:T(8,128)(2,1)}), bf16[16,768,128]{2,1,0:T(8,128)(2,1)}) %all-gather.3.cloned.1.call-update) | async-done | bytes 3145744 | tf_op jit(solution)/shard_map/all_gather | solution.py:83
  152.4 4.7 %copy.16 = bf16[16,768,128]{1,2,0:T(8,128)(2,1)} copy(bf16[16,768,128]{2,1,0:T(8,128)(2,1)} %all-gather.3.cloned.1.call-done) | data formatting | bytes 6291456 | tf_op jit(solution)/shard_map/all_gather | solution.py:83
  157.1 2.0 multiply_reduce_fusion
  159.1 0.6 fusion
  159.7 0.0 copy-done.6
  159.7 0.0 copy-start.1
  159.7 2.5 fusion.11
  162.2 13.4 %all-gather = bf16[64,24,256]{2,1,0:T(8,128)(2,1)S(1)} all-gather(bf16[16,24,256]{2,1,0:T(8,128)(2,1)S(1)} %fusion.11), channel_id=2, replica_groups=mesh['lat'=4,'lon'=32,'tensor'=4] {'tensor'}, dimensions={0}, use_global_device_ids=true | all-gather | bytes 983040 | tf_op jit(solution)/shard_map/all_gather | solution.py:102
  175.6 0.1 reduce_sum.60
  175.7 0.0 copy-done.1
  175.7 0.1 fusion.24
  175.8 1.3 collective-permute-start
  177.1 1.3 collective-permute-start.1
  178.5 0.0 collective-permute-done
  178.5 4.4 %collective-permute-done.1 = bf16[3,24,256]{2,1,0:T(8,128)(2,1)S(1)} collective-permute-done((bf16[3,24,256]{2,1,0:T(8,128)(2,1)S(1)}, bf16[3,24,256]{2,1,0:T(8,128)(2,1)S(1)}, u32[]{:S(2)}, u32[]{:S(2)}) %collective-permute-start.1) | collective-permute-done | bytes 36896 | tf_op jit(solution)/shard_map/ppermute | solution.py:19
  182.9 4.4 %collective-permute-start.2 = (bf16[22,3,256]{2,1,0:T(4,128)(2,1)S(1)}, bf16[22,3,256]{2,1,0:T(4,128)(2,1)S(1)}, u32[]{:S(2)}, u32[]{:S(2)}) collective-permute-start(bf16[22,3,256]{2,1,0:T(4,128)(2,1)S(1)} %get-tuple-element.9), channel_id=1, source_target_pairs={{0,4},{4,8},{8,12},{12,16},{16,20},{20,24},{24,28},{28,32},{32,36}... | collective-permute-start | bytes 101384 | tf_op jit(solution)/shard_map/ppermute | solution.py:18
  187.3 1.9 collective-permute-start.3
  189.3 0.0 collective-permute-done.2
  189.3 4.9 %collective-permute-done.3 = bf16[22,3,256]{2,1,0:T(4,128)(2,1)S(1)} collective-permute-done((bf16[22,3,256]{2,1,0:T(4,128)(2,1)S(1)}, bf16[22,3,256]{2,1,0:T(4,128)(2,1)S(1)}, u32[]{:S(2)}, u32[]{:S(2)}) %collective-permute-start.3) | collective-permute-done | bytes 33824 | tf_op jit(solution)/shard_map/ppermute | solution.py:19
  194.2 0.1 maximum_convert_fusion
  194.3 0.0 copy-start.7
  194.3 0.0 copy-start.5
  194.3 2.9 %convert_reduce_fusion.1 = (f32[16,24]{1,0:T(8,128)S(1)}, bf16[16,24,256]{2,1,0:T(8,128)(2,1)S(1)}) fusion(f32[22,30,256]{2,1,0:T(8,128)S(1)} %maximum_convert_fusion, f32[256]{0:T(256)S(1)} %bitcast.149, f32[256]{0:T(256)S(1)} %bitcast.148, f32[256]{0:T(256)S(1)} %bitcast.147, f32[256]{0:T(256)S(1)} %bitcast.146, f32[256]{0:T(256)S(1)} %bitcast.145, ...), kind=kLoop, calls=%fused_computation.21 | loop fusion | flops 9830016 | bytes 19515904 | tf_op jit(solution)/shard_map/reduce_sum | solution.py:26
  197.2 0.2 fusion.21
  197.5 0.0 copy-done
  197.5 0.0 copy-done.7
  197.5 0.3 fusion.95
  197.9 0.0 copy-done.5
  197.9 0.0 copy-start.4
  197.9 1.8 convolution_convert_fusion.1
  199.7 0.0 all-reduce.2.cloned.1.call-update
  199.7 0.0 copy-done.4
  199.7 55.8 %all-reduce.2.cloned.1.call-done = bf16[16,24,256]{2,1,0:T(8,128)(2,1)} async-done(((bf16[16,24,256]{2,1,0:T(8,128)(2,1)}), bf16[16,24,256]{2,1,0:T(8,128)(2,1)}) %all-reduce.2.cloned.1.call-update) | async-done | bytes 196624 | tf_op jit(solution)/shard_map/psum | solution.py:110
  255.5 1.7 add_convert_fusion
  (16 shorter events, 0.2 us)
Async XLA Ops:
  6.5 191.0 %copy-start = (bf16[256,256]{1,0:T(8,128)(2,1)S(1)}, bf16[256,256]{1,0:T(8,128)(2,1)}, u32[]{:S(2)}) copy-start(bf16[256,256]{1,0:T(8,128)(2,1)} %param.19) | copy-start | bytes 393220
  6.5 5.0 %copy-start.8 = (f32[2]{0:T(128)S(1)}, f32[2]{0:T(128)}, u32[]{:S(2)}) copy-start(f32[2]{0:T(128)} %param.14) | copy-start | bytes 28
  6.5 5.1 %copy-start.2 = (bf16[7,7,256]{2,1,0:T(8,128)(2,1)S(1)}, bf16[7,7,256]{2,1,0:T(8,128)(2,1)}, u32[]{:S(2)}) copy-start(bf16[7,7,256]{2,1,0:T(8,128)(2,1)} %param.17) | copy-start | bytes 75268
  6.5 5.1 %copy-start.3 = (s32[16,256]{1,0:T(8,128)S(1)}, s32[16,256]{1,0:T(8,128)}, u32[]{:S(2)}) copy-start(s32[16,256]{1,0:T(8,128)} %param.16) | copy-start | bytes 49156
  6.5 145.8 %all-gather.3.cloned.1.call-start = ((), (), s32[]{:S(2)}) async-start(), calls=%async_computation | async-start | bytes 3244032 | tf_op jit(solution)/shard_map/all_gather | solution.py:83
  11.5 243.9 %all-reduce.2.cloned.1.call-start = ((), (), s32[]{:S(2)}) async-start(), calls=%async_computation.1 | async-start | bytes 393216 | tf_op jit(solution)/shard_map/psum | solution.py:110
  157.1 2.6 copy-start.6
  159.7 16.1 %copy-start.1 = (bf16[16,24,256]{2,1,0:T(8,128)(2,1)S(1)}, bf16[16,24,256]{2,1,0:T(8,128)(2,1)}, u32[]{:S(2)}) copy-start(bf16[16,24,256]{2,1,0:T(8,128)(2,1)} %param.11) | copy-start | bytes 589828
  175.8 2.6 collective-permute-start
  177.1 5.7 %collective-permute-start.1 = (bf16[3,24,256]{2,1,0:T(8,128)(2,1)S(1)}, bf16[3,24,256]{2,1,0:T(8,128)(2,1)S(1)}, u32[]{:S(2)}, u32[]{:S(2)}) collective-permute-start(bf16[3,24,256]{2,1,0:T(8,128)(2,1)S(1)} %get-tuple-element.12), channel_id=1, source_target_pairs={{128,0},{256,128},{384,256},{129,1},{257,129},{385,257},{130,2},{2... | collective-permute-start | bytes 110600 | tf_op jit(solution)/shard_map/ppermute | solution.py:19
  182.9 6.4 %collective-permute-start.2 = (bf16[22,3,256]{2,1,0:T(4,128)(2,1)S(1)}, bf16[22,3,256]{2,1,0:T(4,128)(2,1)S(1)}, u32[]{:S(2)}, u32[]{:S(2)}) collective-permute-start(bf16[22,3,256]{2,1,0:T(4,128)(2,1)S(1)} %get-tuple-element.9), channel_id=1, source_target_pairs={{0,4},{4,8},{8,12},{12,16},{16,20},{20,24},{24,28},{28,32},{32,36}... | collective-permute-start | bytes 101384 | tf_op jit(solution)/shard_map/ppermute | solution.py:18
  187.3 6.8 %collective-permute-start.3 = (bf16[22,3,256]{2,1,0:T(4,128)(2,1)S(1)}, bf16[22,3,256]{2,1,0:T(4,128)(2,1)S(1)}, u32[]{:S(2)}, u32[]{:S(2)}) collective-permute-start(bf16[22,3,256]{2,1,0:T(4,128)(2,1)S(1)} %get-tuple-element.10), channel_id=1, source_target_pairs={{4,0},{8,4},{12,8},{16,12},{20,16},{24,20},{28,24},{32,28},{36,32}... | collective-permute-start | bytes 101384 | tf_op jit(solution)/shard_map/ppermute | solution.py:19
  194.3 3.2 %copy-start.7 = (f32[256]{0:T(256)S(1)}, f32[256]{0:T(256)}, u32[]{:S(2)}) copy-start(f32[256]{0:T(256)} %param.18) | copy-start | bytes 3076
  194.3 3.6 %copy-start.5 = (bf16[256,256]{1,0:T(8,128)(2,1)S(1)}, bf16[256,256]{1,0:T(8,128)(2,1)}, u32[]{:S(2)}) copy-start(bf16[256,256]{1,0:T(8,128)(2,1)} %param.20) | copy-start | bytes 393220
  197.9 1.8 copy-start.4
Sparse Core Ops, SparseCore 0:
  11.7 140.6 all-gather.2
  199.8 55.6 all-reduce.1
